TPU v7x, 256 devices: a whole 4x4x8 slice. The times are simulated.
256 devices in a mesh: domain: 64 (over z, y, x_lo), band: 4 (over x_hi, core).
Axes of the slice: x: 4 (x_hi: 2, x_lo: 2; x = x_hi * 2 + x_lo), y: 4, z: 8, core: 2. Of those that a mesh axis runs over, the one named last changes fastest.
Arguments:
- orbitals: float32 [128, 131072], P('band', 'domain'), may hold values from -6 to 6
- potential: float32 [131072], P('domain'), may hold values from -1 to 1.5
- cell_scale: float32 [2048], P('domain'), may hold values from 0.5 to 2
- connectivity: int32 [125, 2048], P(None, 'domain'), may hold values from 0 to 2559, as said below
- boundary: int32 [32768], P('domain'), may hold values from 0 to 2047, as said below
Outputs:
- filtered: float32 [128, 131072], P('band', 'domain')
- intersection: float32 [128, 128], P('band')
- projected: float32 [128, 128], P('band')
Inputs may be any that keep to these rules, and one draw needn't show every extreme that they name: `connectivity`: column c lists cell c's nodes in local order 25 c + 5 b + a; a value below 2048 is a node of the cell's own slab, a value 2048 + g is entry g of the next slab's boundary list (the last slab's next is the first); every node of a slab and every such entry is used. `boundary`: each slab's 512 entries are distinct numbers of its own nodes.
All inputs are finite; a program needn't handle non-finite values. Where the computation divides by a largest or mean magnitude, that divisor is 1e-20 or more.
Results may differ from a plain program's by a relative error of at most 0.0001.
Values sent between devices are 32-bit elements; how exact they have to be, the bound alone decides.
A program may use at most 64 MiB of HBM per device.

v0:
```python
import math

import jax
import jax.numpy as jnp
import numpy as np
from jax import lax
from jax.sharding import PartitionSpec as P

DEG = 4


CENTRE = 5.0
SPREAD = 4.0


def passed_along(shard, axis, by):
    count = lax.axis_size(axis)
    return lax.ppermute(shard, axis, [(i, (i + by) % count) for i in range(count)])


def gauss_rule():
    inner = math.sqrt(5.0 - 2.0 * math.sqrt(10.0 / 7.0)) / 3.0
    outer = math.sqrt(5.0 + 2.0 * math.sqrt(10.0 / 7.0)) / 3.0
    w_inner = (322.0 + 13.0 * math.sqrt(70.0)) / 900.0
    w_outer = (322.0 - 13.0 * math.sqrt(70.0)) / 900.0
    points = np.array([-outer, -inner, 0.0, inner, outer])
    weights = np.array([w_outer, w_inner, 128.0 / 225.0, w_inner, w_outer])
    return (points, weights)


def element_matrix():
    nodes_1d = np.linspace(0.0, 1.0, 5)
    points, weights = gauss_rule()
    points = 0.5 * (points + 1.0)
    weights = 0.5 * weights
    values = np.ones((5, 5))
    slopes = np.zeros((5, 5))
    for i in range(5):
        for j in range(5):
            if j != i:
                values[i] = values[i] * (points - nodes_1d[j]) / (nodes_1d[i] - nodes_1d[j])
                product_term = np.ones(5) / (nodes_1d[i] - nodes_1d[j])
                for m in range(5):
                    if m != i and m != j:
                        product_term = (
                            product_term * (points - nodes_1d[m]) / (nodes_1d[i] - nodes_1d[m])
                        )
                slopes[i] = slopes[i] + product_term
    mass_1d = values * weights @ values.T
    stiffness = slopes * weights @ slopes.T
    whole = (
        np.kron(np.kron(stiffness, mass_1d), mass_1d)
        + np.kron(np.kron(mass_1d, stiffness), mass_1d)
        + np.kron(np.kron(mass_1d, mass_1d), stiffness)
    )
    return whole / np.max(np.sum(np.abs(whole), axis=1))


def per_device(orbitals, potential, cell_scale, connectivity, boundary):
    matrix = jnp.asarray(element_matrix(), jnp.float32)
    half_scale = 0.5 * cell_scale
    states_here = orbitals.shape[0]
    nodes_here = orbitals.shape[1]
    cells_here = connectivity.shape[1]
    nodes_total = nodes_here * lax.axis_size("domain")
    flat_links = connectivity.reshape(-1)

    def apply_local(vectors):
        border = jnp.take(vectors, boundary, axis=0)
        beyond = passed_along(border, "domain", -1)
        extended = jnp.concatenate([vectors, beyond], axis=0)
        gathered = jnp.take(extended, flat_links, axis=0).reshape(125, cells_here * states_here)
        products = jnp.dot(matrix, gathered, precision=lax.Precision.HIGHEST).reshape(
            125, cells_here, states_here
        )
        products = products * half_scale[None, :, None]
        summed = (
            jnp.zeros(extended.shape, jnp.float32)
            .at[flat_links]
            .add(products.reshape(125 * cells_here, states_here))
        )
        returned = passed_along(summed[nodes_here:], "domain", 1)
        owned_sums = summed[:nodes_here].at[boundary].add(returned)
        return owned_sums + potential[:, None] * vectors

    start_rows = orbitals.T
    previous = start_rows
    current = (apply_local(start_rows) - CENTRE * start_rows) / SPREAD
    for _ in range(DEG - 1):
        following = 2.0 * (apply_local(current) - CENTRE * current) / SPREAD - previous
        previous, current = (current, following)
    applied = apply_local(current)
    shard_cols = lax.all_gather(current, "band", axis=1, tiled=True)
    intersection_part = jnp.dot(current.T, shard_cols, precision=lax.Precision.HIGHEST)
    image_part = jnp.dot(applied.T, shard_cols, precision=lax.Precision.HIGHEST)
    partial_value = jnp.stack([intersection_part, image_part])
    totals = lax.psum(partial_value, "domain")
    intersection = totals[0] / nodes_total
    projected = totals[1] / nodes_total
    return (current.T, intersection, projected)


def solution(mesh):
    in_specs = (P("band", "domain"), P("domain"), P("domain"), P(None, "domain"), P("domain"))
    out_specs = (P("band", "domain"), P("band", None), P("band", None))
    return jax.shard_map(
        per_device, mesh=mesh, in_specs=in_specs, out_specs=out_specs, check_vma=False
    )
```

profile of v0, /device:TPU:4, one launch (start us, length us, event | category | flops | bytes accessed | tf_op | source)
XLA Modules:
  0.0 705.8 jit_solution(3916110161537922230)
XLA Ops:
  11.1 9.0 %collective-permute-start = (f32[512,32]{1,0:T(8,128)S(1)}, f32[512,32]{1,0:T(8,128)S(1)}, u32[]{:S(2)}, u32[]{:S(2)}) collective-permute-start(f32[512,32]{1,0:T(8,128)S(1)} %broadcast_select_fusion.9), channel_id=1, source_target_pairs={{0,252},{4,0},{8,4},{12,8},{16,12},{20,16},{24,20},{28,24},{32,28}... | collective-permute-start | bytes 196616 | tf_op jit(solution)/shard_map/ppermute | solution.py:18
  20.6 5.1 collective-permute-done
  25.8 14.1 %gather_fusion.1 = f32[4000,32]{1,0:T(8,128)} fusion(f32[2560,32]{1,0:T(8,128)S(1)} %pad_maximum_fusion, s32[4096]{0:T(1024)S(1)} %pad_clamp_fusion), kind=kCustom, calls=%fused_computation.1.clone | custom fusion | bytes 1040000 | tf_op jit(solution)/shard_map/jit(_take)/gather | solution.py:72
  39.9 3.6 broadcast_select_fusion.4
  43.4 1.7 reshape.102
  45.2 2.4 fusion.22
  47.6 1.7 reshape.103
  49.4 25.7 %scatter_custom_fusion = f32[2560,32]{1,0:T(8,128)} fusion(s32[4000]{0:T(1024)S(1)} %bitcast.32, f32[4000,32]{1,0:T(8,128)S(1)} %reshape.103, f32[4000]{0:T(1024)S(1)} %mul.105, f32[]{:T(128)} %constant.26.clone.1), kind=kCustom, calls=%fused_computation.28 | custom fusion | flops 256000 | bytes 2392068 | tf_op jit(solution)/shard_map/scatter-add | solution.py:80
  77.7 10.6 %collective-permute-done.1 = f32[512,32]{1,0:T(8,128)S(1)} collective-permute-done((f32[512,32]{1,0:T(8,128)S(1)}, f32[512,32]{1,0:T(8,128)S(1)}, u32[]{:S(2)}, u32[]{:S(2)}) %collective-permute-start.1) | collective-permute-done | bytes 65568 | tf_op jit(solution)/shard_map/ppermute | solution.py:18
  88.3 3.7 scatter_fusion
  93.3 1.9 collective-permute-start.2
  95.2 4.8 collective-permute-done.2
  101.3 14.1 %gather_fusion.3 = f32[4000,32]{1,0:T(8,128)} fusion(f32[2560,32]{1,0:T(8,128)S(1)} %pad_maximum_fusion.1, s32[4096]{0:T(1024)S(1)} %pad_clamp_fusion), kind=kCustom, calls=%fused_computation.6.clone | custom fusion | bytes 1040000 | tf_op jit(solution)/shard_map/jit(_take)/gather | solution.py:72
  115.4 4.2 broadcast_select_fusion.3
  119.6 2.4 reshape.104
  122.6 2.0 reshape.105
  124.6 25.3 %scatter_custom_fusion.2 = f32[2560,32]{1,0:T(8,128)S(1)} fusion(s32[4000]{0:T(1024)S(1)} %bitcast.33, f32[4000,32]{1,0:T(8,128)} %reshape.105, f32[4000]{0:T(1024)S(1)} %mul.105, f32[]{:T(128)} %constant.26.clone.1), kind=kCustom, calls=%fused_computation.26 | custom fusion | flops 256000 | bytes 856068 | tf_op jit(solution)/shard_map/scatter-add | solution.py:80
  151.5 9.4 %collective-permute-done.3 = f32[512,32]{1,0:T(8,128)} collective-permute-done((f32[512,32]{1,0:T(8,128)S(1)}, f32[512,32]{1,0:T(8,128)}, u32[]{:S(2)}, u32[]{:S(2)}) %collective-permute-start.3) | collective-permute-done | bytes 65568 | tf_op jit(solution)/shard_map/ppermute | solution.py:18
  160.9 5.6 scatter_fusion.1
  169.1 1.8 collective-permute-start.4
  170.9 4.9 collective-permute-done.4
  175.9 14.1 %gather_fusion.5 = f32[4000,32]{1,0:T(8,128)} fusion(f32[2560,32]{1,0:T(8,128)S(1)} %pad_maximum_fusion.2, s32[4096]{0:T(1024)S(1)} %pad_clamp_fusion), kind=kCustom, calls=%fused_computation.7.clone | custom fusion | bytes 1040000 | tf_op jit(solution)/shard_map/jit(_take)/gather | solution.py:72
  190.0 4.2 broadcast_select_fusion.2
  194.2 2.4 reshape.106
  197.2 2.0 reshape.107
  199.2 25.3 %scatter_custom_fusion.4 = f32[2560,32]{1,0:T(8,128)S(1)} fusion(s32[4000]{0:T(1024)S(1)} %bitcast.34, f32[4000,32]{1,0:T(8,128)} %reshape.107, f32[4000]{0:T(1024)S(1)} %mul.105, f32[]{:T(128)} %constant.26.clone.1), kind=kCustom, calls=%fused_computation.24 | custom fusion | flops 256000 | bytes 856068 | tf_op jit(solution)/shard_map/scatter-add | solution.py:80
  226.0 9.4 %collective-permute-done.5 = f32[512,32]{1,0:T(8,128)S(1)} collective-permute-done((f32[512,32]{1,0:T(8,128)S(1)}, f32[512,32]{1,0:T(8,128)S(1)}, u32[]{:S(2)}, u32[]{:S(2)}) %collective-permute-start.5) | collective-permute-done | bytes 65568 | tf_op jit(solution)/shard_map/ppermute | solution.py:18
  235.3 5.2 scatter_fusion.2
  243.1 1.9 collective-permute-start.6
  245.0 5.0 collective-permute-done.6
  250.1 14.1 %gather_fusion.7 = f32[4000,32]{1,0:T(8,128)} fusion(f32[2560,32]{1,0:T(8,128)S(1)} %pad_maximum_fusion.3, s32[4096]{0:T(1024)S(1)} %pad_clamp_fusion), kind=kCustom, calls=%fused_computation.8.clone | custom fusion | bytes 1040000 | tf_op jit(solution)/shard_map/jit(_take)/gather | solution.py:72
  264.1 4.2 broadcast_select_fusion.1
  268.3 2.4 reshape.108
  271.4 2.0 reshape.109
  273.4 25.3 %scatter_custom_fusion.6 = f32[2560,32]{1,0:T(8,128)S(1)} fusion(s32[4000]{0:T(1024)S(1)} %bitcast.35, f32[4000,32]{1,0:T(8,128)} %reshape.109, f32[4000]{0:T(1024)S(1)} %mul.105, f32[]{:T(128)} %constant.26.clone.1), kind=kCustom, calls=%fused_computation.22 | custom fusion | flops 256000 | bytes 856068 | tf_op jit(solution)/shard_map/scatter-add | solution.py:80
  300.2 9.3 %collective-permute-done.7 = f32[512,32]{1,0:T(8,128)} collective-permute-done((f32[512,32]{1,0:T(8,128)S(1)}, f32[512,32]{1,0:T(8,128)}, u32[]{:S(2)}, u32[]{:S(2)}) %collective-permute-start.7) | collective-permute-done | bytes 65568 | tf_op jit(solution)/shard_map/ppermute | solution.py:18
  309.5 5.6 scatter_fusion.3
  321.4 2.9 collective-permute-done.8
  324.4 14.1 %gather_fusion.9 = f32[4000,32]{1,0:T(8,128)} fusion(f32[2560,32]{1,0:T(8,128)S(1)} %pad_maximum_fusion.4, s32[4096]{0:T(1024)S(1)} %pad_clamp_fusion), kind=kCustom, calls=%fused_computation.9.clone | custom fusion | bytes 1040000 | tf_op jit(solution)/shard_map/jit(_take)/gather | solution.py:72
  338.5 3.6 broadcast_select_fusion
  343.8 2.4 fusion.26
  346.2 1.7 reshape.111
  348.0 25.7 %scatter_custom_fusion.8 = f32[2560,32]{1,0:T(8,128)} fusion(s32[4000]{0:T(1024)S(1)} %bitcast.36, f32[4000,32]{1,0:T(8,128)S(1)} %reshape.111, f32[4000]{0:T(1024)S(1)} %mul.105, f32[]{:T(128)} %constant.26.clone.1), kind=kCustom, calls=%fused_computation.20 | custom fusion | flops 256000 | bytes 2392068 | tf_op jit(solution)/shard_map/scatter-add | solution.py:80
  376.3 9.0 %collective-permute-done.9 = f32[512,32]{1,0:T(8,128)S(1)} collective-permute-done((f32[512,32]{1,0:T(8,128)S(1)}, f32[512,32]{1,0:T(8,128)S(1)}, u32[]{:S(2)}, u32[]{:S(2)}) %collective-permute-start.9) | collective-permute-done | bytes 65568 | tf_op jit(solution)/shard_map/ppermute | solution.py:18
  385.3 3.9 scatter_fusion.4
  389.2 3.1 convolution_bitcast_fusion.1
  392.3 1.8 convolution_bitcast_fusion
  394.1 304.1 %psum.7 = f32[2,32,128]{2,1,0:T(8,128)S(1)} all-reduce(f32[2,32,128]{2,1,0:T(8,128)S(1)} %pad_maximum_fusion.5), channel_id=1, replica_groups=mesh['domain'=64,'band'=4] {'domain'}, use_global_device_ids=true, to_apply=%region_10.13 | all-reduce | flops 8192 | bytes 65536 | tf_op jit(solution)/shard_map/psum | solution.py:97
  (83 shorter events, 32.3 us)
Async XLA Ops:
  7.2 382.0 %all-gather.2.cloned.1.call-start = ((), (), s32[]{:S(2)}) async-start(), calls=%async_computation | async-start | bytes 1310720 | tf_op jit(solution)/shard_map/all_gather | solution.py:93
  8.6 11.5 %copy-start.9 = (s32[125,32]{0,1:T(8,128)S(1)}, s32[125,32]{0,1:T(8,128)}, u32[]{:S(2)}) copy-start(s32[125,32]{0,1:T(8,128)} %param.13) | copy-start | bytes 48004
  8.6 11.9 %copy-start.10 = (f32[32]{0:T(128)S(1)}, f32[32]{0:T(128)}, u32[]{:S(2)}) copy-start(f32[32]{0:T(128)} %param.12) | copy-start | bytes 388
  11.1 14.6 %collective-permute-start = (f32[512,32]{1,0:T(8,128)S(1)}, f32[512,32]{1,0:T(8,128)S(1)}, u32[]{:S(2)}, u32[]{:S(2)}) collective-permute-start(f32[512,32]{1,0:T(8,128)S(1)} %broadcast_select_fusion.9), channel_id=1, source_target_pairs={{0,252},{4,0},{8,4},{12,8},{16,12},{20,16},{24,20},{28,24},{32,28}... | collective-permute-start | bytes 196616 | tf_op jit(solution)/shard_map/ppermute | solution.py:18
  43.4 1.8 copy-start.7
  49.4 26.7 %copy-start.8 = (f32[2048]{0:T(1024)S(1)}, f32[2048]{0:T(1024)}, u32[]{:S(2)}) copy-start(f32[2048]{0:T(1024)} %param.11) | copy-start | bytes 24580
  76.0 12.3 %collective-permute-start.1 = (f32[512,32]{1,0:T(8,128)S(1)}, f32[512,32]{1,0:T(8,128)S(1)}, u32[]{:S(2)}, u32[]{:S(2)}) collective-permute-start(f32[512,32]{1,0:T(8,128)S(1)} %slice.69), channel_id=1, source_target_pairs={{0,4},{4,8},{8,12},{12,16},{16,20},{20,24},{24,28},{28,32},{32,36}... | collective-permute-start | bytes 196616 | tf_op jit(solution)/shard_map/ppermute | solution.py:18
  92.0 58.2 %copy-start.2 = (f32[2048,32]{1,0:T(8,128)}, f32[2048,32]{1,0:T(8,128)S(1)}, u32[]{:S(2)}) copy-start(f32[2048,32]{1,0:T(8,128)S(1)} %scatter_fusion) | copy-start | bytes 786436
  92.1 3.1 copy-start.4
  93.3 6.7 collective-permute-start.2
  150.0 10.9 %collective-permute-start.3 = (f32[512,32]{1,0:T(8,128)S(1)}, f32[512,32]{1,0:T(8,128)}, u32[]{:S(2)}, u32[]{:S(2)}) collective-permute-start(f32[512,32]{1,0:T(8,128)S(1)} %slice.71), channel_id=1, source_target_pairs={{0,4},{4,8},{8,12},{12,16},{16,20},{20,24},{24,28},{28,32},{32,36}... | collective-permute-start | bytes 196616 | tf_op jit(solution)/shard_map/ppermute | solution.py:18
  151.5 15.0 %copy-start.3 = (f32[2048,32]{1,0:T(8,128)S(1)}, f32[2048,32]{1,0:T(8,128)}, u32[]{:S(2)}) copy-start(f32[2048,32]{1,0:T(8,128)} %copy-done.2) | copy-start | bytes 786436
  169.1 6.7 collective-permute-start.4
  224.6 10.8 %collective-permute-start.5 = (f32[512,32]{1,0:T(8,128)S(1)}, f32[512,32]{1,0:T(8,128)S(1)}, u32[]{:S(2)}, u32[]{:S(2)}) collective-permute-start(f32[512,32]{1,0:T(8,128)S(1)} %slice.73), channel_id=1, source_target_pairs={{0,4},{4,8},{8,12},{12,16},{16,20},{20,24},{24,28},{28,32},{32,36}... | collective-permute-start | bytes 196616 | tf_op jit(solution)/shard_map/ppermute | solution.py:18
  226.0 14.6 %copy-start.5 = (f32[2048,32]{1,0:T(8,128)S(1)}, f32[2048,32]{1,0:T(8,128)}, u32[]{:S(2)}) copy-start(f32[2048,32]{1,0:T(8,128)} %copy-done.4) | copy-start | bytes 786436
  241.9 56.9 %copy-start = (f32[2048,32]{1,0:T(8,128)}, f32[2048,32]{1,0:T(8,128)S(1)}, u32[]{:S(2)}) copy-start(f32[2048,32]{1,0:T(8,128)S(1)} %multiply_subtract_fusion.1) | copy-start | bytes 786436
  243.1 6.9 collective-permute-start.6
  298.8 10.8 %collective-permute-start.7 = (f32[512,32]{1,0:T(8,128)S(1)}, f32[512,32]{1,0:T(8,128)}, u32[]{:S(2)}, u32[]{:S(2)}) collective-permute-start(f32[512,32]{1,0:T(8,128)S(1)} %slice.75), channel_id=1, source_target_pairs={{0,4},{4,8},{8,12},{12,16},{16,20},{20,24},{24,28},{28,32},{32,36}... | collective-permute-start | bytes 196616 | tf_op jit(solution)/shard_map/ppermute | solution.py:18
  300.2 14.9 %copy-start.1 = (f32[2048,32]{1,0:T(8,128)S(1)}, f32[2048,32]{1,0:T(8,128)}, u32[]{:S(2)}) copy-start(f32[2048,32]{1,0:T(8,128)} %copy-done) | copy-start | bytes 786436
  317.7 6.6 collective-permute-start.8
  374.6 10.7 %collective-permute-start.9 = (f32[512,32]{1,0:T(8,128)S(1)}, f32[512,32]{1,0:T(8,128)S(1)}, u32[]{:S(2)}, u32[]{:S(2)}) collective-permute-start(f32[512,32]{1,0:T(8,128)S(1)} %slice.77), channel_id=1, source_target_pairs={{0,4},{4,8},{8,12},{12,16},{16,20},{20,24},{24,28},{28,32},{32,36}... | collective-permute-start | bytes 196616 | tf_op jit(solution)/shard_map/ppermute | solution.py:18
  389.2 3.1 copy-start.6
Sparse Core Ops, SparseCore 0:
  320.5 15.1 all-gather.1
where the time goes:
time: 715 us; the launch traced here: 706 us
  blocking collectives  304 us (43%)
  other arithmetic  187 us (26%)
  local copies, waits for them, and re-layouts  102 us (14%)
  waiting for transfers between devices  70.5 us (10%)
  starting transfers between devices  16.6 us (2%)
  between operations  14.8 us (2%)
  matrix products  11.4 us (2%)
    psum x1, blocking collectives, per_device(): totals = lax.psum(partial_value, 'domain')  304 us
    scatter-add x5, other arithmetic, apply_local(): summed = jnp.zeros(extended.shape, jnp.float32).at[flat_links].add(produc...  127 us
    ppermute x10, waiting for transfers between devices, passed_along(): lax.ppermute(shard, axis, [(i, (i + by) % count) for i in range(count)])  70.4 us
    gather x5, local copies, waits for them, and re-layouts, apply_local(): jnp.take(extended, flat_links, axis=0)  70.4 us
    scatter-add x5, other arithmetic, apply_local(): owned_sums = summed[:nodes_here].at[boundary].add(returned)  23.9 us
    select_n x6, other arithmetic, apply_local(): jnp.take(extended, flat_links, axis=0)  19.8 us
    ppermute x10, starting transfers between devices, passed_along(): lax.ppermute(shard, axis, [(i, (i + by) % count) for i in range(count)])  16.6 us
  transfers between devices with their start and end apart: 11, of which 10 were waited for; matrix products, arithmetic and copies ran while one was open for 9% of the time, Pallas kernels for 0%

commit v1 on v0

v1 whole, which is shorter than its diff:
```python
import math

import jax
import jax.numpy as jnp
import numpy as np
from jax import lax
from jax.experimental import pallas as pl
from jax.experimental.pallas import tpu as pltpu
from jax.sharding import PartitionSpec as P

DEG = 4
CENTRE = 5.0
SPREAD = 4.0
MESH = pl.DeviceIdType.MESH
F32 = jnp.float32
BF16 = jnp.bfloat16
F8 = jnp.float8_e4m3fn
PIECES = 4
STEP = 32.0
TOP = 128.0
LOC = 128
CHUNK = 512


def gauss_rule():
    inner = math.sqrt(5.0 - 2.0 * math.sqrt(10.0 / 7.0)) / 3.0
    outer = math.sqrt(5.0 + 2.0 * math.sqrt(10.0 / 7.0)) / 3.0
    w_inner = (322.0 + 13.0 * math.sqrt(70.0)) / 900.0
    w_outer = (322.0 - 13.0 * math.sqrt(70.0)) / 900.0
    points = np.array([-outer, -inner, 0.0, inner, outer])
    weights = np.array([w_outer, w_inner, 128.0 / 225.0, w_inner, w_outer])
    return (points, weights)


def element_matrix():
    nodes_1d = np.linspace(0.0, 1.0, 5)
    points, weights = gauss_rule()
    points = 0.5 * (points + 1.0)
    weights = 0.5 * weights
    values = np.ones((5, 5))
    slopes = np.zeros((5, 5))
    for i in range(5):
        for j in range(5):
            if j != i:
                values[i] = values[i] * (points - nodes_1d[j]) / (nodes_1d[i] - nodes_1d[j])
                product_term = np.ones(5) / (nodes_1d[i] - nodes_1d[j])
                for m in range(5):
                    if m != i and m != j:
                        product_term = (
                            product_term * (points - nodes_1d[m]) / (nodes_1d[i] - nodes_1d[m])
                        )
                slopes[i] = slopes[i] + product_term
    mass_1d = values * weights @ values.T
    stiffness = slopes * weights @ slopes.T
    whole = (
        np.kron(np.kron(stiffness, mass_1d), mass_1d)
        + np.kron(np.kron(mass_1d, stiffness), mass_1d)
        + np.kron(np.kron(mass_1d, mass_1d), stiffness)
    )
    return whole / np.max(np.sum(np.abs(whole), axis=1))


def element_tile():
    matrix = np.zeros((LOC, LOC), np.float32)
    matrix[:125, :125] = element_matrix().T.astype(np.float32)
    high = matrix.astype(jnp.bfloat16)
    low = (matrix - high.astype(np.float32)).astype(jnp.bfloat16)
    row = np.concatenate([high, low], axis=1)
    return np.concatenate([row, row], axis=0)


def dot(a, b):
    return jnp.dot(a, b, preferred_element_type=F32)


def row_max(x):
    return jnp.maximum(jnp.max(jnp.abs(x), axis=1, keepdims=True), 1e-30)


def cut(x, inverse):
    rest = x * inverse
    pieces = []
    for p in range(PIECES):
        piece = rest.astype(F8)
        pieces.append(piece)
        if p < PIECES - 1:
            rest = (rest - piece.astype(F32)) * STEP
    return pieces


def joined(d, scale, states):
    total = d[(PIECES - 1) * states :]
    for p in range(PIECES - 2, -1, -1):
        total = d[p * states : (p + 1) * states] + total * (1.0 / STEP)
    return total * scale


def kernel(
    n_domain, n_band, nodes_total,
    orb, pot, scl, conn, bnd, kk,
    filt_out, inter_out, proj_out,
    gt, gs, gpt, gps, bt, bs, cpad, pack, packp,
    cur, old, ay, pv, pb, pg, pr, pw, wo, xs, r2,
    bsend, grecv, rsend, rrecv,
    fall, lhs, rhs, part, rsrecv, zbuf, tot,
    pk_ss, pk_rs, b_ss, b_rs, r_ss, r_rs, f_ss, f_rs, s1_ss, s1_rs, s2_ss, s2_rs, s3_ss, s3_rs,
):
    states, nodes = orb.shape
    cells = conn.shape[1]
    ghosts = bnd.shape[0] * bnd.shape[1]
    width = cells * LOC
    per = CHUNK // LOC
    me = lax.axis_index("domain")
    mb = lax.axis_index("band")
    nxt = lax.rem(me + 1, n_domain)
    prv = lax.rem(me + n_domain - 1, n_domain)
    near = mb + 1 - 2 * lax.rem(mb, 2)
    far = lax.rem(mb + 2, n_band)
    q = lax.rem(me, 8)
    z = me // 8
    zs = n_domain // 8
    base = z * 8

    barrier = pltpu.get_barrier_semaphore()

    def greet(where):
        pl.semaphore_signal(barrier, inc=1, device_id=where, device_id_type=MESH)

    greet({"domain": nxt})
    greet({"domain": prv})
    greet({"band": near})
    greet({"band": far})
    for r in range(1, 8):
        greet({"domain": base + lax.rem(q + r, 8)})
    for r in range(1, zs):
        greet({"domain": lax.rem(z + r, zs) * 8 + q})
    greeted = 4 + 7 + zs - 1

    def copy(src, dst, ss, rs, where):
        return pltpu.make_async_remote_copy(
            src_ref=src, dst_ref=dst, send_sem=ss, recv_sem=rs, device_id=where, device_id_type=MESH
        )

    cpad[...] = jnp.full(cpad.shape, -1.0, F32)
    cpad[0 : conn.shape[0], 0:cells] = conn[...].astype(F32)
    pack[0:cells, :] = cpad[...].T[0:cells, :]
    eye = lax.broadcasted_iota(jnp.int32, (cells, cells), 0) == lax.broadcasted_iota(
        jnp.int32, (cells, cells), 1
    )
    factors = jnp.sum(jnp.where(eye, scl[...], 0.0), axis=1, keepdims=True) * 0.5
    pack[cells : 2 * cells, :] = jnp.broadcast_to(factors, (cells, LOC))

    down = lax.broadcasted_iota(jnp.int32, (32, LOC), 0).astype(F32)
    across = lax.broadcasted_iota(jnp.int32, (LOC, LOC), 1).astype(F32)

    def one_hot_t(dst, lanes, row, first, count):
        delta = row - down
        for n in range(0, count, 32):
            dst[n : n + 32, lanes] = jnp.where(delta == float(first + n), 1.0, 0.0).astype(F8)

    def one_hot(dst, rows, row, first, count):
        delta = jnp.broadcast_to(row, (LOC, LOC)).T - across
        for n in range(0, count, LOC):
            dst[rows, n : n + LOC] = jnp.where(delta == float(first + n), 1.0, 0.0).astype(F8)

    for g in range(ghosts // LOC):
        row = bnd[g : g + 1, :].astype(F32)
        one_hot_t(bt, slice(g * LOC, (g + 1) * LOC), row, 0, nodes)
        one_hot(bs, slice(g * LOC, (g + 1) * LOC), row, 0, nodes)

    pl.semaphore_wait(barrier, greeted)
    pack_copy = copy(pack, packp, pk_ss, pk_rs, {"domain": nxt})
    pack_copy.start()

    @pl.loop(0, cells)
    def _(c):
        span = pl.ds(pl.multiple_of(c * LOC, LOC), LOC)
        row = pack[pl.ds(c, 1), :]
        one_hot_t(gt, span, row, 0, nodes + ghosts)
        one_hot(gs, span, row, 0, nodes + ghosts)

    pack_copy.wait()

    @pl.loop(0, cells)
    def _(c):
        span = pl.ds(pl.multiple_of(c * LOC, LOC), LOC)
        row = packp[pl.ds(c, 1), :]
        one_hot_t(gpt, span, row, nodes, ghosts)
        one_hot(gps, span, row, nodes, ghosts)

    cur[...] = orb[...]
    old[...] = orb[...]

    def put(dst, at, pieces):
        for p in range(PIECES):
            dst[p * states : (p + 1) * states, at] = pieces[p]

    def cell_products(d, scale, factor_rows, c0):
        u = joined(d, scale, states)
        for i in range(per):
            one = u[:, i * LOC : (i + 1) * LOC]
            high = one.astype(BF16)
            at = slice((c0 + i) * states, (c0 + i + 1) * states)
            xs[at, 0:LOC] = high
            xs[at, LOC : 2 * LOC] = (one - high.astype(F32)).astype(BF16)
        both = dot(xs[c0 * states : (c0 + per) * states, :], kk[...])
        out = []
        for i in range(per):
            at = slice(i * states, (i + 1) * states)
            out.append((both[at, 0:LOC] + both[at, LOC:]) * factor_rows[c0 + i : c0 + i + 1, :])
        return out

    def application(k, gather):
        y = cur[...]
        top = row_max(y)
        scale, inverse = top * (1.0 / TOP), TOP / top
        put(pv, slice(0, nodes), cut(y, inverse))
        d = dot(pv[...], bt[...])
        pb[...] = d.astype(F8)
        bsend[k] = joined(d, scale, states)
        border = copy(bsend.at[k], grecv.at[k], b_ss.at[k], b_rs.at[k], {"domain": prv})
        border.start()
        if gather:
            f_near = copy(cur, fall.at[mb], f_ss.at[0], f_rs.at[0], {"band": near})
            f_far = copy(cur, fall.at[mb], f_ss.at[1], f_rs.at[1], {"band": far})
            f_near.start()
            f_far.start()

        own = pack.at[cells : 2 * cells, :]
        for n in range(0, width, CHUNK):
            d = dot(pv[...], gt[0:nodes, n : n + CHUNK])
            for i, w in enumerate(cell_products(d, scale, own, n // LOC)):
                at = slice(n + i * LOC, n + (i + 1) * LOC)
                wo[:, at] = w
                put(pw, at, cut(w, inverse))
        rsend[k] = joined(dot(pw[...], gs[:, nodes:]), scale, states)
        back = copy(rsend.at[k], rrecv.at[k], r_ss.at[k], r_rs.at[k], {"domain": nxt})
        back.start()

        before = packp.at[cells : 2 * cells, :]
        for n in range(0, width, CHUNK):
            d = dot(pb[...], gpt[:, n : n + CHUNK])
            for i, w in enumerate(cell_products(d, scale, before, n // LOC)):
                put(pw, slice(n + i * LOC, n + (i + 1) * LOC), cut(w, inverse))
        r2[...] = joined(dot(pw[...], gps[...]), scale, states)

        border.wait()
        ghost = grecv[k]
        top_g = row_max(ghost)
        scale_g, inverse_g = top_g * (1.0 / TOP), TOP / top_g
        put(pg, slice(0, ghosts), cut(ghost, inverse_g))
        both = jnp.maximum(top, top_g)
        scale_b, inverse_b = both * (1.0 / TOP), TOP / both
        for n in range(0, width, CHUNK):
            d = dot(pg[...], gt[nodes:, n : n + CHUNK])
            for i, w in enumerate(cell_products(d, scale_g, own, n // LOC)):
                at = slice(n + i * LOC, n + (i + 1) * LOC)
                put(pw, at, cut(wo[:, at] + w, inverse_b))
        for n in range(0, nodes, CHUNK):
            at = slice(n, n + CHUNK)
            ay[:, at] = joined(dot(pw[...], gs[:, at]), scale_b, states)
        if gather:
            f_near.wait()
            f_far.wait()
            f_pass = copy(fall.at[far], fall.at[far], f_ss.at[2], f_rs.at[2], {"band": near})
            f_pass.start()
        back.wait()
        shared = rrecv[k] + r2[...]
        top_r = row_max(shared)
        put(pr, slice(0, ghosts), cut(shared, TOP / top_r))
        for n in range(0, nodes, CHUNK):
            at = slice(n, n + CHUNK)
            ay[:, at] = ay[:, at] + joined(dot(pr[...], bs[:, at]), top_r * (1.0 / TOP), states)
        for t in range(nodes // LOC):
            at = slice(t * LOC, (t + 1) * LOC)
            ay[:, at] = ay[:, at] + pot[t : t + 1, :] * cur[:, at]
        return f_pass if gather else None

    @pl.loop(0, DEG)
    def _(k):
        application(k, False)
        first = (k == 0).astype(F32)
        alpha = (2.0 - first) / SPREAD
        beta = 1.0 - first
        y = cur[...]
        following = alpha * (ay[...] - CENTRE * y) - beta * old[...]
        old[...] = y
        cur[...] = following

    f_pass = application(DEG, True)
    filt_out[...] = cur[...]
    fall[mb] = cur[...]
    for i, value in enumerate((cur, ay)):
        v = value[...]
        high = v.astype(BF16)
        lhs[2 * i * states : (2 * i + 1) * states, :] = high
        lhs[(2 * i + 1) * states : (2 * i + 2) * states, :] = (v - high.astype(F32)).astype(BF16)
    f_pass.wait()
    everyone = n_band * states
    for j in range(n_band):
        v = fall[j]
        high = v.astype(BF16)
        rhs[j * states : (j + 1) * states, :] = high
        rhs[everyone + j * states : everyone + (j + 1) * states, :] = (v - high.astype(F32)).astype(BF16)
    g = lax.dot_general(
        lhs[...], rhs[...], (((1,), (1,)), ((), ())), preferred_element_type=F32
    )
    g = g[:, :everyone] + g[:, everyone:]
    part[0 : states // 8] = (g[0:states] + g[states : 2 * states]).reshape(states // 8, 8, everyone)
    part[states // 8 :] = (g[2 * states : 3 * states] + g[3 * states :]).reshape(
        states // 8, 8, everyone
    )

    sends = []
    for r in range(1, 8):
        peer = lax.rem(q + r, 8)
        c = copy(part.at[peer], rsrecv.at[r], s1_ss.at[r], s1_rs.at[r], {"domain": base + peer})
        c.start()
        sends.append(c)
    for c in sends:
        c.wait()
    total = part[q]
    for r in range(1, 8):
        total = total + rsrecv[r]
    zbuf[z] = total
    sends = []
    for r in range(1, zs):
        peer = lax.rem(z + r, zs)
        c = copy(zbuf.at[z], zbuf.at[z], s2_ss.at[r], s2_rs.at[r], {"domain": peer * 8 + q})
        c.start()
        sends.append(c)
    for c in sends:
        c.wait()
    total = zbuf[0]
    for r in range(1, zs):
        total = total + zbuf[r]
    tot[q] = total * (1.0 / nodes_total)
    sends = []
    for r in range(1, 8):
        peer = lax.rem(q + r, 8)
        c = copy(tot.at[q], tot.at[q], s3_ss.at[r], s3_rs.at[r], {"domain": base + peer})
        c.start()
        sends.append(c)
    for c in sends:
        c.wait()
    inter_out[...] = tot[0 : states // 8].reshape(states, everyone)
    proj_out[...] = tot[states // 8 :].reshape(states, everyone)


def solution(mesh):
    n_domain, n_band = mesh.shape["domain"], mesh.shape["band"]
    tile = element_tile()

    def per_device(orbitals, potential, cell_scale, connectivity, boundary):
        states, nodes = orbitals.shape
        cells = connectivity.shape[1]
        ghosts = boundary.shape[0]
        width = cells * LOC
        rows = PIECES * states
        everyone = n_band * states
        vm = pltpu.VMEM
        dma = pltpu.SemaphoreType.DMA
        body = lambda *refs: kernel(n_domain, n_band, nodes * n_domain, *refs)
        return pl.pallas_call(
            body,
            name="chebyshev_step",
            out_shape=(
                jax.ShapeDtypeStruct((states, nodes), F32),
                jax.ShapeDtypeStruct((states, everyone), F32),
                jax.ShapeDtypeStruct((states, everyone), F32),
            ),
            in_specs=[pl.BlockSpec(memory_space=vm)] * 6,
            out_specs=(pl.BlockSpec(memory_space=vm),) * 3,
            scratch_shapes=[
                vm((nodes + ghosts, width), F8),
                vm((width, nodes + ghosts), F8),
                vm((ghosts, width), F8),
                vm((width, ghosts), F8),
                vm((nodes, ghosts), F8),
                vm((ghosts, nodes), F8),
                vm((LOC, LOC), F32),
                vm((2 * cells, LOC), F32),
                vm((2 * cells, LOC), F32),
                vm((states, nodes), F32),
                vm((states, nodes), F32),
                vm((states, nodes), F32),
                vm((rows, nodes), F8),
                vm((rows, ghosts), F8),
                vm((rows, ghosts), F8),
                vm((rows, ghosts), F8),
                vm((rows, width), F8),
                vm((states, width), F32),
                vm((cells * states, 2 * LOC), BF16),
                vm((states, ghosts), F32),
                vm((DEG + 1, states, ghosts), F32),
                vm((DEG + 1, states, ghosts), F32),
                vm((DEG + 1, states, ghosts), F32),
                vm((DEG + 1, states, ghosts), F32),
                vm((n_band, states, nodes), F32),
                vm((4 * states, nodes), BF16),
                vm((2 * everyone, nodes), BF16),
                vm((8, 8, everyone), F32),
                vm((8, 8, everyone), F32),
                vm((n_domain // 8, 8, everyone), F32),
                vm((8, 8, everyone), F32),
                dma, dma,
                dma((DEG + 1,)), dma((DEG + 1,)), dma((DEG + 1,)), dma((DEG + 1,)),
                dma((3,)), dma((3,)),
                dma((8,)), dma((8,)), dma((n_domain // 8,)), dma((n_domain // 8,)), dma((8,)), dma((8,)),
            ],
            compiler_params=pltpu.CompilerParams(
                collective_id=0, has_side_effects=True, vmem_limit_bytes=60 * 2**20
            ),
        )(
            orbitals,
            potential.reshape(nodes // LOC, LOC),
            cell_scale.reshape(1, cells),
            connectivity,
            boundary.reshape(ghosts // LOC, LOC),
            jnp.asarray(tile),
        )

    in_specs = (P("band", "domain"), P("domain"), P("domain"), P(None, "domain"), P("domain"))
    out_specs = (P("band", "domain"), P("band", None), P("band", None))
    return jax.shard_map(
        per_device, mesh=mesh, in_specs=in_specs, out_specs=out_specs, check_vma=False
    )
```

time: 715 us -> 85.5 us (0.12); the launches traced: 706 us -> 85.3 us
  blocking collectives: 304 us -> 0 us
  other arithmetic: 187 us -> 0 us
  local copies, waits for them, and re-layouts: 102 us -> 4.46 us
  Pallas kernels: 0 us -> 80.2 us
  waiting for transfers between devices: 70.5 us -> 0 us
  starting transfers between devices: 16.6 us -> 0 us
  between operations: 14.8 us -> 0.65 us
  matrix products: 11.4 us -> 0 us
    psum x1 -> x0, blocking collectives: 304 us -> none  [per_device(): totals = lax.psum(partial_value, 'domain')]
    scatter-add x10 -> x0, other arithmetic: 151 us -> none  [the longest x5 127 us: apply_local(): summed = jnp.zeros(extended.shape, jnp.float32).at[flat_links].add(produc...]
    pallas_call x0 -> x1, Pallas kernels: none -> 80.2 us  [per_device(): pl.pallas_call(body, name='chebyshev_step', out_shape=(jax.ShapeDtypeStru...]
    gather x10 -> x0, local copies, waits for them, and re-layouts: 75.6 us -> none  [the longest x5 70.4 us: apply_local(): jnp.take(extended, flat_links, axis=0)]
    ppermute x10 -> x0, waiting for transfers between devices: 70.4 us -> none  [passed_along(): lax.ppermute(shard, axis, [(i, (i + by) % count) for i in range(count)])]
    select_n x13 -> x0, other arithmetic: 21.1 us -> none  [the longest x6 19.8 us: apply_local(): jnp.take(extended, flat_links, axis=0)]
    reshape x12 -> x0, local copies, waits for them, and re-layouts: 20.4 us -> none  [the longest x5 10.8 us: apply_local(): jnp.take(extended, flat_links, axis=0)]
    ppermute x10 -> x0, starting transfers between devices: 16.6 us -> none  [passed_along(): lax.ppermute(shard, axis, [(i, (i + by) % count) for i in range(count)])]
  transfers between devices with their start and end apart: 11 -> 0, of which waited for: 10 -> 0; matrix products, arithmetic and copies ran while one was open for 9% -> 0% of each run, Pallas kernels for 0% -> 0%
where the time goes in v1:
time: 85.5 us; the launch traced here: 85.3 us
  Pallas kernels  80.2 us (94%)
  local copies, waits for them, and re-layouts  4.46 us (5%)
    pallas_call x1, Pallas kernels, per_device(): pl.pallas_call(body, name='chebyshev_step', out_shape=(jax.ShapeDtypeStru...  80.2 us
    unnamed x8, local copies, waits for them, and re-layouts  4.46 us

profile of v1, /device:TPU:4, one launch (start us, length us, event | category | flops | bytes accessed | tf_op | source)
XLA Modules:
  0.0 85.3 jit_solution(9021846182328923592)
XLA Ops:
  0.6 1.5 %copy.9.refs_3_ = s32[125,32]{1,0:T(8,128)} copy(s32[125,32]{0,1:T(8,128)} %param.9) | data formatting | bytes 32000 | tf_op args[3]
  2.1 80.2 %chebyshev_step.1 = (f32[32,2048]{1,0:T(8,128)}, f32[32,128]{1,0:T(8,128)}, f32[32,128]{1,0:T(8,128)}) custom-call(f32[32,2048]{1,0:T(8,128)} %refs_0_.1, f32[16,128]{1,0:T(8,128)} %bitcast.3, f32[1,32]{1,0:T(1,128)} %bitcast.5, s32[125,32]{1,0:T(8,128)} %copy.9.refs_3_, s32[4,128]{1,0:T(4,128)} %bitcast.4, bf16[256,256]{1,0:T(8,128)(2,1)} %constant.2.clone.refs_5_), custom_call_target="tpu_custom_call" | custom-call | tf_op jit(solution)/shard_map/chebyshev_step/pallas_call | solution.py:364
  82.2 0.0 copy-start.1
  82.3 1.7 %copy.13 = f32[32,2048]{1,0:T(8,128)} copy(f32[32,2048]{1,0:T(8,128)} %get-tuple-element.6) | data formatting | bytes 524288
  83.9 0.0 copy-done.1
  83.9 0.0 copy-start
  83.9 0.6 copy.14
  84.5 0.1 copy-done
  84.7 0.6 copy.15
Async XLA Ops:
  82.2 1.7 %copy-start.1 = (f32[32,128]{1,0:T(8,128)S(1)}, f32[32,128]{1,0:T(8,128)}, u32[]{:S(2)}) copy-start(f32[32,128]{1,0:T(8,128)} %get-tuple-element.7) | copy-start | bytes 49156
  83.9 0.7 copy-start

commit v2 on v1

--- a/solution.py
+++ b/solution.py
@@ -98,18 +98,17 @@
 def kernel(
     n_domain, n_band, nodes_total,
     orb, pot, scl, conn, bnd, kk,
-    filt_out, inter_out, proj_out,
-    gt, gs, gpt, gps, bt, bs, cpad, pack, packp,
-    cur, old, ay, pv, pb, pg, pr, pw, wo, xs, r2,
+    filt_out, total_out,
+    gt, gs, gpt, gps, bt, bs, pack, packp,
+    cur, old, ay, pv, pb, pg, pr, pw, pwp, wo, xs, xsp, r2,
     bsend, grecv, rsend, rrecv,
     fall, lhs, rhs, part, rsrecv, zbuf, tot,
-    pk_ss, pk_rs, b_ss, b_rs, r_ss, r_rs, f_ss, f_rs, s1_ss, s1_rs, s2_ss, s2_rs, s3_ss, s3_rs,
+    out_s, pk_ss, pk_rs, b_ss, b_rs, r_ss, r_rs, f_ss, f_rs, s1_ss, s1_rs, s2_ss, s2_rs, s3_ss, s3_rs,
 ):
     states, nodes = orb.shape
-    cells = conn.shape[1]
+    cells = conn.shape[0]
     ghosts = bnd.shape[0] * bnd.shape[1]
     width = cells * LOC
-    per = CHUNK // LOC
     me = lax.axis_index("domain")
     mb = lax.axis_index("band")
     nxt = lax.rem(me + 1, n_domain)
@@ -141,52 +140,45 @@
             src_ref=src, dst_ref=dst, send_sem=ss, recv_sem=rs, device_id=where, device_id_type=MESH
         )
 
-    cpad[...] = jnp.full(cpad.shape, -1.0, F32)
-    cpad[0 : conn.shape[0], 0:cells] = conn[...].astype(F32)
-    pack[0:cells, :] = cpad[...].T[0:cells, :]
+    pack[0:cells, :] = jnp.full((cells, LOC), -1.0, F32)
+    pack[0:cells, 0 : conn.shape[1]] = conn[...].astype(F32)
     eye = lax.broadcasted_iota(jnp.int32, (cells, cells), 0) == lax.broadcasted_iota(
         jnp.int32, (cells, cells), 1
     )
     factors = jnp.sum(jnp.where(eye, scl[...], 0.0), axis=1, keepdims=True) * 0.5
     pack[cells : 2 * cells, :] = jnp.broadcast_to(factors, (cells, LOC))
 
-    down = lax.broadcasted_iota(jnp.int32, (32, LOC), 0).astype(F32)
+    down = lax.broadcasted_iota(jnp.int32, (LOC, LOC), 0).astype(F32)
     across = lax.broadcasted_iota(jnp.int32, (LOC, LOC), 1).astype(F32)
-
-    def one_hot_t(dst, lanes, row, first, count):
-        delta = row - down
-        for n in range(0, count, 32):
-            dst[n : n + 32, lanes] = jnp.where(delta == float(first + n), 1.0, 0.0).astype(F8)
-
-    def one_hot(dst, rows, row, first, count):
-        delta = jnp.broadcast_to(row, (LOC, LOC)).T - across
-        for n in range(0, count, LOC):
-            dst[rows, n : n + LOC] = jnp.where(delta == float(first + n), 1.0, 0.0).astype(F8)
+    nothing = jnp.zeros((LOC, LOC), F8)
+
+    def one_hot(upright, flat, span, row, first, count):
+        block = jnp.floor(row * (1.0 / LOC))
+        rest = jnp.broadcast_to(row - block * LOC, (LOC, LOC))
+        block = jnp.broadcast_to(block, (LOC, LOC))
+        hot_u = jnp.where(rest == down, 1.0, 0.0).astype(F8)
+        hot_f = jnp.where(rest.T == across, 1.0, 0.0).astype(F8)
+        block_u = block.astype(jnp.int32).astype(jnp.int8)
+        block_f = block.T.astype(jnp.int32).astype(jnp.int8)
+        for t in range(count // LOC):
+            at = slice(t * LOC, (t + 1) * LOC)
+            now = jnp.int8(first // LOC + t)
+            upright[at, span] = jnp.where(block_u == now, hot_u, nothing)
+            flat[span, at] = jnp.where(block_f == now, hot_f, nothing)
+
+    def own_matrices(lo, hi):
+        @pl.loop(lo, hi, unroll=4)
+        def _(c):
+            span = pl.ds(pl.multiple_of(c * LOC, LOC), LOC)
+            one_hot(gt, gs, span, pack[pl.ds(c, 1), :], 0, nodes + ghosts)
 
     for g in range(ghosts // LOC):
-        row = bnd[g : g + 1, :].astype(F32)
-        one_hot_t(bt, slice(g * LOC, (g + 1) * LOC), row, 0, nodes)
-        one_hot(bs, slice(g * LOC, (g + 1) * LOC), row, 0, nodes)
-
+        one_hot(bt, bs, slice(g * LOC, (g + 1) * LOC), bnd[g : g + 1, :].astype(F32), 0, nodes)
+    own_matrices(0, cells // 2)
     pl.semaphore_wait(barrier, greeted)
     pack_copy = copy(pack, packp, pk_ss, pk_rs, {"domain": nxt})
     pack_copy.start()
-
-    @pl.loop(0, cells)
-    def _(c):
-        span = pl.ds(pl.multiple_of(c * LOC, LOC), LOC)
-        row = pack[pl.ds(c, 1), :]
-        one_hot_t(gt, span, row, 0, nodes + ghosts)
-        one_hot(gs, span, row, 0, nodes + ghosts)
-
-    pack_copy.wait()
-
-    @pl.loop(0, cells)
-    def _(c):
-        span = pl.ds(pl.multiple_of(c * LOC, LOC), LOC)
-        row = packp[pl.ds(c, 1), :]
-        one_hot_t(gpt, span, row, nodes, ghosts)
-        one_hot(gps, span, row, nodes, ghosts)
+    own_matrices(cells // 2, cells)
 
     cur[...] = orb[...]
     old[...] = orb[...]
@@ -195,22 +187,35 @@
         for p in range(PIECES):
             dst[p * states : (p + 1) * states, at] = pieces[p]
 
-    def cell_products(d, scale, factor_rows, c0):
-        u = joined(d, scale, states)
-        for i in range(per):
-            one = u[:, i * LOC : (i + 1) * LOC]
-            high = one.astype(BF16)
-            at = slice((c0 + i) * states, (c0 + i + 1) * states)
-            xs[at, 0:LOC] = high
-            xs[at, LOC : 2 * LOC] = (one - high.astype(F32)).astype(BF16)
-        both = dot(xs[c0 * states : (c0 + per) * states, :], kk[...])
-        out = []
-        for i in range(per):
-            at = slice(i * states, (i + 1) * states)
-            out.append((both[at, 0:LOC] + both[at, LOC:]) * factor_rows[c0 + i : c0 + i + 1, :])
-        return out
-
-    def application(k, gather):
+    def gathered(values, upright, rows, scale, dst):
+        for n in range(0, width, CHUNK):
+            u = joined(dot(values[...], upright[rows, n : n + CHUNK]), scale, states)
+            for i in range(CHUNK // LOC):
+                one = u[:, i * LOC : (i + 1) * LOC]
+                high = one.astype(BF16)
+                at = slice((n // LOC + i) * states, (n // LOC + i + 1) * states)
+                dst[at, 0:LOC] = high
+                dst[at, LOC : 2 * LOC] = (one - high.astype(F32)).astype(BF16)
+
+    def cell_products(src, factor_rows, use):
+        for c0 in range(0, cells, 8):
+            both = dot(src[c0 * states : (c0 + 8) * states, :], kk[...])
+            for i in range(8):
+                at = slice(i * states, (i + 1) * states)
+                use(
+                    slice((c0 + i) * LOC, (c0 + i + 1) * LOC),
+                    (both[at, 0:LOC] + both[at, LOC:]) * factor_rows[c0 + i : c0 + i + 1, :],
+                )
+
+    own = pack.at[cells : 2 * cells, :]
+    before = packp.at[cells : 2 * cells, :]
+    f_near = copy(fall.at[mb], fall.at[mb], f_ss.at[0], f_rs.at[0], {"band": near})
+    f_far = copy(fall.at[mb], fall.at[mb], f_ss.at[1], f_rs.at[1], {"band": far})
+    f_pass = copy(fall.at[far], fall.at[far], f_ss.at[2], f_rs.at[2], {"band": near})
+    f_out = pltpu.make_async_copy(fall.at[mb], filt_out, out_s)
+
+    @pl.loop(0, DEG + 1)
+    def _(k):
         y = cur[...]
         top = row_max(y)
         scale, inverse = top * (1.0 / TOP), TOP / top
@@ -220,29 +225,37 @@
         bsend[k] = joined(d, scale, states)
         border = copy(bsend.at[k], grecv.at[k], b_ss.at[k], b_rs.at[k], {"domain": prv})
         border.start()
-        if gather:
-            f_near = copy(cur, fall.at[mb], f_ss.at[0], f_rs.at[0], {"band": near})
-            f_far = copy(cur, fall.at[mb], f_ss.at[1], f_rs.at[1], {"band": far})
+
+        @pl.when(k == DEG)
+        def _():
+            fall[mb] = cur[...]
             f_near.start()
             f_far.start()
-
-        own = pack.at[cells : 2 * cells, :]
-        for n in range(0, width, CHUNK):
-            d = dot(pv[...], gt[0:nodes, n : n + CHUNK])
-            for i, w in enumerate(cell_products(d, scale, own, n // LOC)):
-                at = slice(n + i * LOC, n + (i + 1) * LOC)
-                wo[:, at] = w
-                put(pw, at, cut(w, inverse))
+            f_out.start()
+
+        gathered(pv, gt, slice(0, nodes), scale, xs)
+
+        def keep(at, w):
+            wo[:, at] = w
+            put(pw, at, cut(w, inverse))
+
+        cell_products(xs, own, keep)
         rsend[k] = joined(dot(pw[...], gs[:, nodes:]), scale, states)
         back = copy(rsend.at[k], rrecv.at[k], r_ss.at[k], r_rs.at[k], {"domain": nxt})
         back.start()
 
-        before = packp.at[cells : 2 * cells, :]
-        for n in range(0, width, CHUNK):
-            d = dot(pb[...], gpt[:, n : n + CHUNK])
-            for i, w in enumerate(cell_products(d, scale, before, n // LOC)):
-                put(pw, slice(n + i * LOC, n + (i + 1) * LOC), cut(w, inverse))
-        r2[...] = joined(dot(pw[...], gps[...]), scale, states)
+        @pl.when(k == 0)
+        def _():
+            pack_copy.wait()
+
+            @pl.loop(0, cells, unroll=4)
+            def _(c):
+                span = pl.ds(pl.multiple_of(c * LOC, LOC), LOC)
+                one_hot(gpt, gps, span, packp[pl.ds(c, 1), :], nodes, ghosts)
+
+        gathered(pb, gpt, slice(0, ghosts), scale, xsp)
+        cell_products(xsp, before, lambda at, w: put(pwp, at, cut(w, inverse)))
+        r2[...] = joined(dot(pwp[...], gps[...]), scale, states)
 
         border.wait()
         ghost = grecv[k]
@@ -251,46 +264,38 @@
         put(pg, slice(0, ghosts), cut(ghost, inverse_g))
         both = jnp.maximum(top, top_g)
         scale_b, inverse_b = both * (1.0 / TOP), TOP / both
-        for n in range(0, width, CHUNK):
-            d = dot(pg[...], gt[nodes:, n : n + CHUNK])
-            for i, w in enumerate(cell_products(d, scale_g, own, n // LOC)):
-                at = slice(n + i * LOC, n + (i + 1) * LOC)
-                put(pw, at, cut(wo[:, at] + w, inverse_b))
+        gathered(pg, gt, slice(nodes, nodes + ghosts), scale_g, xs)
+        cell_products(xs, own, lambda at, w: put(pw, at, cut(wo[:, at] + w, inverse_b)))
         for n in range(0, nodes, CHUNK):
             at = slice(n, n + CHUNK)
             ay[:, at] = joined(dot(pw[...], gs[:, at]), scale_b, states)
-        if gather:
+
+        @pl.when(k == DEG)
+        def _():
             f_near.wait()
             f_far.wait()
-            f_pass = copy(fall.at[far], fall.at[far], f_ss.at[2], f_rs.at[2], {"band": near})
             f_pass.start()
+
         back.wait()
         shared = rrecv[k] + r2[...]
         top_r = row_max(shared)
         put(pr, slice(0, ghosts), cut(shared, TOP / top_r))
-        for n in range(0, nodes, CHUNK):
-            at = slice(n, n + CHUNK)
-            ay[:, at] = ay[:, at] + joined(dot(pr[...], bs[:, at]), top_r * (1.0 / TOP), states)
-        for t in range(nodes // LOC):
-            at = slice(t * LOC, (t + 1) * LOC)
-            ay[:, at] = ay[:, at] + pot[t : t + 1, :] * cur[:, at]
-        return f_pass if gather else None
-
-    @pl.loop(0, DEG)
-    def _(k):
-        application(k, False)
         first = (k == 0).astype(F32)
         alpha = (2.0 - first) / SPREAD
         beta = 1.0 - first
-        y = cur[...]
-        following = alpha * (ay[...] - CENTRE * y) - beta * old[...]
-        old[...] = y
-        cur[...] = following
-
-    f_pass = application(DEG, True)
-    filt_out[...] = cur[...]
-    fall[mb] = cur[...]
-    for i, value in enumerate((cur, ay)):
+        for n in range(0, nodes, CHUNK):
+            h = joined(dot(pr[...], bs[:, n : n + CHUNK]), top_r * (1.0 / TOP), states)
+            for i in range(CHUNK // LOC):
+                at = slice(n + i * LOC, n + (i + 1) * LOC)
+                t = n // LOC + i
+                v = cur[:, at]
+                full = ay[:, at] + h[:, i * LOC : (i + 1) * LOC] + pot[t : t + 1, :] * v
+                ay[:, at] = full
+                cur[:, at] = alpha * (full - CENTRE * v) - beta * old[:, at]
+                old[:, at] = v
+
+    f_out.wait()
+    for i, value in enumerate((old, ay)):
         v = value[...]
         high = v.astype(BF16)
         lhs[2 * i * states : (2 * i + 1) * states, :] = high
@@ -343,8 +348,14 @@
         sends.append(c)
     for c in sends:
         c.wait()
-    inter_out[...] = tot[0 : states // 8].reshape(states, everyone)
-    proj_out[...] = tot[states // 8 :].reshape(states, everyone)
+    total_out[...] = tot[...].reshape(2 * states, everyone)
+
+
+def write_out(filt, total, filt_out, inter_out, proj_out):
+    states = filt.shape[0]
+    filt_out[...] = filt[...]
+    inter_out[...] = total[0:states, :]
+    proj_out[...] = total[states:, :]
 
 
 def solution(mesh):
@@ -361,16 +372,15 @@
         vm = pltpu.VMEM
         dma = pltpu.SemaphoreType.DMA
         body = lambda *refs: kernel(n_domain, n_band, nodes * n_domain, *refs)
-        return pl.pallas_call(
+        filtered, totals = pl.pallas_call(
             body,
             name="chebyshev_step",
             out_shape=(
                 jax.ShapeDtypeStruct((states, nodes), F32),
-                jax.ShapeDtypeStruct((states, everyone), F32),
-                jax.ShapeDtypeStruct((states, everyone), F32),
+                jax.ShapeDtypeStruct((2 * states, everyone), F32),
             ),
             in_specs=[pl.BlockSpec(memory_space=vm)] * 6,
-            out_specs=(pl.BlockSpec(memory_space=vm),) * 3,
+            out_specs=(pl.BlockSpec(memory_space=pl.ANY), pl.BlockSpec(memory_space=vm)),
             scratch_shapes=[
                 vm((nodes + ghosts, width), F8),
                 vm((width, nodes + ghosts), F8),
@@ -378,7 +388,6 @@
                 vm((width, ghosts), F8),
                 vm((nodes, ghosts), F8),
                 vm((ghosts, nodes), F8),
-                vm((LOC, LOC), F32),
                 vm((2 * cells, LOC), F32),
                 vm((2 * cells, LOC), F32),
                 vm((states, nodes), F32),
@@ -389,7 +398,9 @@
                 vm((rows, ghosts), F8),
                 vm((rows, ghosts), F8),
                 vm((rows, width), F8),
+                vm((rows, width), F8),
                 vm((states, width), F32),
+                vm((cells * states, 2 * LOC), BF16),
                 vm((cells * states, 2 * LOC), BF16),
                 vm((states, ghosts), F32),
                 vm((DEG + 1, states, ghosts), F32),
@@ -403,7 +414,7 @@
                 vm((8, 8, everyone), F32),
                 vm((n_domain // 8, 8, everyone), F32),
                 vm((8, 8, everyone), F32),
-                dma, dma,
+                dma, dma, dma,
                 dma((DEG + 1,)), dma((DEG + 1,)), dma((DEG + 1,)), dma((DEG + 1,)),
                 dma((3,)), dma((3,)),
                 dma((8,)), dma((8,)), dma((n_domain // 8,)), dma((n_domain // 8,)), dma((8,)), dma((8,)),
@@ -415,10 +426,21 @@
             orbitals,
             potential.reshape(nodes // LOC, LOC),
             cell_scale.reshape(1, cells),
-            connectivity,
+            connectivity.T,
             boundary.reshape(ghosts // LOC, LOC),
             jnp.asarray(tile),
         )
+        return pl.pallas_call(
+            write_out,
+            name="outputs",
+            out_shape=(
+                jax.ShapeDtypeStruct((states, nodes), F32),
+                jax.ShapeDtypeStruct((states, everyone), F32),
+                jax.ShapeDtypeStruct((states, everyone), F32),
+            ),
+            in_specs=[pl.BlockSpec(memory_space=vm)] * 2,
+            out_specs=(pl.BlockSpec(memory_space=vm),) * 3,
+        )(filtered, totals)
 
     in_specs = (P("band", "domain"), P("domain"), P("domain"), P(None, "domain"), P("domain"))
     out_specs = (P("band", "domain"), P("band", None), P("band", None))

time: 85.5 us -> 69.1 us (0.81)
  Pallas kernels: 80.2 us -> 68.4 us
  local copies, waits for them, and re-layouts: 4.46 us -> 0 us
    pallas_call x1, Pallas kernels: 80.2 us -> 66.7 us  [per_device(): pl.pallas_call(body, name='chebyshev_step', out_shape=(jax.ShapeDtypeStru...]
    unnamed x8 -> x0, local copies, waits for them, and re-layouts: 4.46 us -> none
    pallas_call x0 -> x1, Pallas kernels: none -> 1.68 us  [per_device(): pl.pallas_call(write_out, name='outputs', out_shape=(jax.ShapeDtypeStruct...]
where the time goes in v2:
time: 69.1 us; the launch traced here: 69 us
  Pallas kernels  68.4 us (99%)
    pallas_call x1, Pallas kernels, per_device(): pl.pallas_call(body, name='chebyshev_step', out_shape=(jax.ShapeDtypeStru...  66.7 us
    pallas_call x1, Pallas kernels, per_device(): pl.pallas_call(write_out, name='outputs', out_shape=(jax.ShapeDtypeStruct...  1.68 us

profile of v2, /device:TPU:4, one launch (start us, length us, event | category | flops | bytes accessed | tf_op | source)
XLA Modules:
  0.0 69.0 jit_solution(8037702819698752596)
XLA Ops:
  0.6 66.7 %chebyshev_step.1 = (f32[32,2048]{1,0:T(8,128)}, f32[64,128]{1,0:T(8,128)}) custom-call(f32[32,2048]{1,0:T(8,128)} %refs_0_.1, f32[16,128]{1,0:T(8,128)} %bitcast.5, f32[1,32]{1,0:T(1,128)} %bitcast.7, s32[32,125]{1,0:T(8,128)} %bitcast.4, s32[4,128]{1,0:T(4,128)} %bitcast.6, bf16[256,256]{1,0:T(8,128)(2,1)} %constant.2.clone.refs_5_), custom_call_target="tpu_custom_call" | custom-call | tf_op jit(solution)/shard_map/chebyshev_step/pallas_call | solution.py:375
  67.3 1.7 %outputs.1 = (f32[32,2048]{1,0:T(8,128)}, f32[32,128]{1,0:T(8,128)}, f32[32,128]{1,0:T(8,128)}) custom-call(f32[32,2048]{1,0:T(8,128)} %get-tuple-element.5.filt, f32[64,128]{1,0:T(8,128)} %get-tuple-element.6.total), custom_call_target="tpu_custom_call" | custom-call | tf_op jit(solution)/shard_map/outputs/pallas_call | solution.py:433

commit v3 on v2

--- a/solution.py
+++ b/solution.py
@@ -210,8 +210,22 @@
     own = pack.at[cells : 2 * cells, :]
     before = packp.at[cells : 2 * cells, :]
     f_near = copy(fall.at[mb], fall.at[mb], f_ss.at[0], f_rs.at[0], {"band": near})
-    f_far = copy(fall.at[mb], fall.at[mb], f_ss.at[1], f_rs.at[1], {"band": far})
-    f_pass = copy(fall.at[far], fall.at[far], f_ss.at[2], f_rs.at[2], {"band": near})
+    halves = [slice(0, nodes // 2), slice(nodes // 2, nodes)]
+    f_far = [
+        copy(fall.at[mb, :, h], fall.at[mb, :, h], f_ss.at[1 + i], f_rs.at[1 + i], {"band": far})
+        for i, h in enumerate(halves)
+    ]
+    f_pass = [
+        copy(fall.at[far, :, h], fall.at[far, :, h], f_ss.at[3 + i], f_rs.at[3 + i], {"band": near})
+        for i, h in enumerate(halves)
+    ]
+
+    def border_copy(k):
+        return copy(bsend.at[k], grecv.at[k], b_ss.at[k], b_rs.at[k], {"domain": prv})
+
+    def back_copy(k):
+        return copy(rsend.at[k], rrecv.at[k], r_ss.at[k], r_rs.at[k], {"domain": nxt})
+
     f_out = pltpu.make_async_copy(fall.at[mb], filt_out, out_s)
 
     @pl.loop(0, DEG + 1)
@@ -223,14 +237,14 @@
         d = dot(pv[...], bt[...])
         pb[...] = d.astype(F8)
         bsend[k] = joined(d, scale, states)
-        border = copy(bsend.at[k], grecv.at[k], b_ss.at[k], b_rs.at[k], {"domain": prv})
-        border.start()
+        border_copy(k).start()
 
         @pl.when(k == DEG)
         def _():
             fall[mb] = cur[...]
             f_near.start()
-            f_far.start()
+            f_far[0].start()
+            f_far[1].start()
             f_out.start()
 
         gathered(pv, gt, slice(0, nodes), scale, xs)
@@ -241,8 +255,7 @@
 
         cell_products(xs, own, keep)
         rsend[k] = joined(dot(pw[...], gs[:, nodes:]), scale, states)
-        back = copy(rsend.at[k], rrecv.at[k], r_ss.at[k], r_rs.at[k], {"domain": nxt})
-        back.start()
+        back_copy(k).start()
 
         @pl.when(k == 0)
         def _():
@@ -257,7 +270,7 @@
         cell_products(xsp, before, lambda at, w: put(pwp, at, cut(w, inverse)))
         r2[...] = joined(dot(pwp[...], gps[...]), scale, states)
 
-        border.wait()
+        border_copy(k).wait_recv()
         ghost = grecv[k]
         top_g = row_max(ghost)
         scale_g, inverse_g = top_g * (1.0 / TOP), TOP / top_g
@@ -272,11 +285,10 @@
 
         @pl.when(k == DEG)
         def _():
-            f_near.wait()
-            f_far.wait()
-            f_pass.start()
-
-        back.wait()
+            f_far[0].wait_recv()
+            f_pass[0].start()
+
+        back_copy(k).wait_recv()
         shared = rrecv[k] + r2[...]
         top_r = row_max(shared)
         put(pr, slice(0, ghosts), cut(shared, TOP / top_r))
@@ -294,13 +306,16 @@
                 cur[:, at] = alpha * (full - CENTRE * v) - beta * old[:, at]
                 old[:, at] = v
 
-    f_out.wait()
+    f_far[1].wait_recv()
+    f_pass[1].start()
     for i, value in enumerate((old, ay)):
         v = value[...]
         high = v.astype(BF16)
         lhs[2 * i * states : (2 * i + 1) * states, :] = high
         lhs[(2 * i + 1) * states : (2 * i + 2) * states, :] = (v - high.astype(F32)).astype(BF16)
-    f_pass.wait()
+    f_near.wait_recv()
+    f_pass[0].wait_recv()
+    f_pass[1].wait_recv()
     everyone = n_band * states
     for j in range(n_band):
         v = fall[j]
@@ -316,14 +331,15 @@
         states // 8, 8, everyone
     )
 
-    sends = []
+    sends, sent = [], []
     for r in range(1, 8):
         peer = lax.rem(q + r, 8)
         c = copy(part.at[peer], rsrecv.at[r], s1_ss.at[r], s1_rs.at[r], {"domain": base + peer})
         c.start()
         sends.append(c)
     for c in sends:
-        c.wait()
+        c.wait_recv()
+    sent += sends
     total = part[q]
     for r in range(1, 8):
         total = total + rsrecv[r]
@@ -335,7 +351,8 @@
         c.start()
         sends.append(c)
     for c in sends:
-        c.wait()
+        c.wait_recv()
+    sent += sends
     total = zbuf[0]
     for r in range(1, zs):
         total = total + zbuf[r]
@@ -347,8 +364,15 @@
         c.start()
         sends.append(c)
     for c in sends:
-        c.wait()
+        c.wait_recv()
+    sent += sends
     total_out[...] = tot[...].reshape(2 * states, everyone)
+    for k in range(DEG + 1):
+        border_copy(k).wait_send()
+        back_copy(k).wait_send()
+    for c in sent + [f_near] + f_far + f_pass:
+        c.wait_send()
+    f_out.wait()
 
 
 def write_out(filt, total, filt_out, inter_out, proj_out):
@@ -416,7 +440,7 @@
                 vm((8, 8, everyone), F32),
                 dma, dma, dma,
                 dma((DEG + 1,)), dma((DEG + 1,)), dma((DEG + 1,)), dma((DEG + 1,)),
-                dma((3,)), dma((3,)),
+                dma((5,)), dma((5,)),
                 dma((8,)), dma((8,)), dma((n_domain // 8,)), dma((n_domain // 8,)), dma((8,)), dma((8,)),
             ],
             compiler_params=pltpu.CompilerParams(

time: 69.1 us -> 69.4 us (level)
  no operation moved by 1% of the time
where the time goes in v3:
time: 69.4 us; the launch traced here: 69.2 us
  Pallas kernels  68.6 us (99%)
    pallas_call x1, Pallas kernels, per_device(): pl.pallas_call(body, name='chebyshev_step', out_shape=(jax.ShapeDtypeStru...  66.9 us
    pallas_call x1, Pallas kernels, per_device(): pl.pallas_call(write_out, name='outputs', out_shape=(jax.ShapeDtypeStruct...  1.68 us

profile of v3, /device:TPU:4, one launch (start us, length us, event | category | flops | bytes accessed | tf_op | source)
XLA Modules:
  0.0 69.2 jit_solution(10090849962488681540)
XLA Ops:
  0.6 66.9 %chebyshev_step.1 = (f32[32,2048]{1,0:T(8,128)}, f32[64,128]{1,0:T(8,128)}) custom-call(f32[32,2048]{1,0:T(8,128)} %refs_0_.1, f32[16,128]{1,0:T(8,128)} %bitcast.5, f32[1,32]{1,0:T(1,128)} %bitcast.7, s32[32,125]{1,0:T(8,128)} %bitcast.4, s32[4,128]{1,0:T(4,128)} %bitcast.6, bf16[256,256]{1,0:T(8,128)(2,1)} %constant.2.clone.refs_5_), custom_call_target="tpu_custom_call" | custom-call | tf_op jit(solution)/shard_map/chebyshev_step/pallas_call | solution.py:399
  67.6 1.7 %outputs.1 = (f32[32,2048]{1,0:T(8,128)}, f32[32,128]{1,0:T(8,128)}, f32[32,128]{1,0:T(8,128)}) custom-call(f32[32,2048]{1,0:T(8,128)} %get-tuple-element.5.filt, f32[64,128]{1,0:T(8,128)} %get-tuple-element.6.total), custom_call_target="tpu_custom_call" | custom-call | tf_op jit(solution)/shard_map/outputs/pallas_call | solution.py:457

commit v4 on v3

--- a/solution.py
+++ b/solution.py
@@ -16,10 +16,12 @@
 BF16 = jnp.bfloat16
 F8 = jnp.float8_e4m3fn
 PIECES = 4
+PRODUCT_PIECES = 3
 STEP = 32.0
 TOP = 128.0
 LOC = 128
 CHUNK = 512
+PART = 8
 
 
 def gauss_rule():
@@ -77,22 +79,22 @@
     return jnp.maximum(jnp.max(jnp.abs(x), axis=1, keepdims=True), 1e-30)
 
 
-def cut(x, inverse):
-    rest = x * inverse
+def cut(x, count):
     pieces = []
-    for p in range(PIECES):
-        piece = rest.astype(F8)
+    for p in range(count):
+        piece = x.astype(F8)
         pieces.append(piece)
-        if p < PIECES - 1:
-            rest = (rest - piece.astype(F32)) * STEP
+        if p < count - 1:
+            x = (x - piece.astype(F32)) * STEP
     return pieces
 
 
-def joined(d, scale, states):
-    total = d[(PIECES - 1) * states :]
-    for p in range(PIECES - 2, -1, -1):
+def joined(d, count):
+    states = d.shape[0] // count
+    total = d[(count - 1) * states :]
+    for p in range(count - 2, -1, -1):
         total = d[p * states : (p + 1) * states] + total * (1.0 / STEP)
-    return total * scale
+    return total
 
 
 def kernel(
@@ -184,12 +186,12 @@
     old[...] = orb[...]
 
     def put(dst, at, pieces):
-        for p in range(PIECES):
-            dst[p * states : (p + 1) * states, at] = pieces[p]
-
-    def gathered(values, upright, rows, scale, dst):
-        for n in range(0, width, CHUNK):
-            u = joined(dot(values[...], upright[rows, n : n + CHUNK]), scale, states)
+        for p, piece in enumerate(pieces):
+            dst[p * states : (p + 1) * states, at] = piece
+
+    def gathered(values, upright, rows, dst, lo, hi):
+        for n in range(lo * LOC, hi * LOC, CHUNK):
+            u = joined(dot(values[...], upright[rows, n : n + CHUNK]), PIECES)
             for i in range(CHUNK // LOC):
                 one = u[:, i * LOC : (i + 1) * LOC]
                 high = one.astype(BF16)
@@ -197,15 +199,19 @@
                 dst[at, 0:LOC] = high
                 dst[at, LOC : 2 * LOC] = (one - high.astype(F32)).astype(BF16)
 
-    def cell_products(src, factor_rows, use):
-        for c0 in range(0, cells, 8):
-            both = dot(src[c0 * states : (c0 + 8) * states, :], kk[...])
-            for i in range(8):
-                at = slice(i * states, (i + 1) * states)
-                use(
-                    slice((c0 + i) * LOC, (c0 + i + 1) * LOC),
-                    (both[at, 0:LOC] + both[at, LOC:]) * factor_rows[c0 + i : c0 + i + 1, :],
-                )
+    def cell_products(src, factor_rows, use, lo, hi):
+        both = dot(src[lo * states : hi * states, :], kk[...])
+        for i in range(hi - lo):
+            at = slice(i * states, (i + 1) * states)
+            use(
+                slice((lo + i) * LOC, (lo + i + 1) * LOC),
+                (both[at, 0:LOC] + both[at, LOC:]) * factor_rows[lo + i : lo + i + 1, :],
+            )
+
+    def elements(values, upright, rows, dst, factor_rows, use):
+        gathered(values, upright, rows, dst, 0, cells)
+        for c in range(0, cells, PART):
+            cell_products(dst, factor_rows, use, c, c + PART)
 
     own = pack.at[cells : 2 * cells, :]
     before = packp.at[cells : 2 * cells, :]
@@ -233,10 +239,10 @@
         y = cur[...]
         top = row_max(y)
         scale, inverse = top * (1.0 / TOP), TOP / top
-        put(pv, slice(0, nodes), cut(y, inverse))
+        put(pv, slice(0, nodes), cut(y * inverse, PIECES))
         d = dot(pv[...], bt[...])
         pb[...] = d.astype(F8)
-        bsend[k] = joined(d, scale, states)
+        bsend[k] = joined(d, PIECES) * scale
         border_copy(k).start()
 
         @pl.when(k == DEG)
@@ -247,14 +253,12 @@
             f_far[1].start()
             f_out.start()
 
-        gathered(pv, gt, slice(0, nodes), scale, xs)
-
         def keep(at, w):
             wo[:, at] = w
-            put(pw, at, cut(w, inverse))
-
-        cell_products(xs, own, keep)
-        rsend[k] = joined(dot(pw[...], gs[:, nodes:]), scale, states)
+            put(pw, at, cut(w, PRODUCT_PIECES))
+
+        elements(pv, gt, slice(0, nodes), xs, own, keep)
+        rsend[k] = joined(dot(pw[...], gs[:, nodes:]), PRODUCT_PIECES) * scale
         back_copy(k).start()
 
         @pl.when(k == 0)
@@ -266,22 +270,25 @@
                 span = pl.ds(pl.multiple_of(c * LOC, LOC), LOC)
                 one_hot(gpt, gps, span, packp[pl.ds(c, 1), :], nodes, ghosts)
 
-        gathered(pb, gpt, slice(0, ghosts), scale, xsp)
-        cell_products(xsp, before, lambda at, w: put(pwp, at, cut(w, inverse)))
-        r2[...] = joined(dot(pwp[...], gps[...]), scale, states)
+        elements(
+            pb, gpt, slice(0, ghosts), xsp, before,
+            lambda at, w: put(pwp, at, cut(w, PRODUCT_PIECES)),
+        )
+        r2[...] = joined(dot(pwp[...], gps[...]), PRODUCT_PIECES) * scale
 
         border_copy(k).wait_recv()
         ghost = grecv[k]
         top_g = row_max(ghost)
-        scale_g, inverse_g = top_g * (1.0 / TOP), TOP / top_g
-        put(pg, slice(0, ghosts), cut(ghost, inverse_g))
+        put(pg, slice(0, ghosts), cut(ghost * (TOP / top_g), PIECES))
         both = jnp.maximum(top, top_g)
-        scale_b, inverse_b = both * (1.0 / TOP), TOP / both
-        gathered(pg, gt, slice(nodes, nodes + ghosts), scale_g, xs)
-        cell_products(xs, own, lambda at, w: put(pw, at, cut(wo[:, at] + w, inverse_b)))
+        ratio, ratio_g, scale_b = top / both, top_g / both, both * (1.0 / TOP)
+        elements(
+            pg, gt, slice(nodes, nodes + ghosts), xs, own,
+            lambda at, w: put(pw, at, cut(wo[:, at] * ratio + w * ratio_g, PRODUCT_PIECES)),
+        )
         for n in range(0, nodes, CHUNK):
             at = slice(n, n + CHUNK)
-            ay[:, at] = joined(dot(pw[...], gs[:, at]), scale_b, states)
+            ay[:, at] = joined(dot(pw[...], gs[:, at]), PRODUCT_PIECES) * scale_b
 
         @pl.when(k == DEG)
         def _():
@@ -291,12 +298,12 @@
         back_copy(k).wait_recv()
         shared = rrecv[k] + r2[...]
         top_r = row_max(shared)
-        put(pr, slice(0, ghosts), cut(shared, TOP / top_r))
+        put(pr, slice(0, ghosts), cut(shared * (TOP / top_r), PIECES))
         first = (k == 0).astype(F32)
         alpha = (2.0 - first) / SPREAD
         beta = 1.0 - first
         for n in range(0, nodes, CHUNK):
-            h = joined(dot(pr[...], bs[:, n : n + CHUNK]), top_r * (1.0 / TOP), states)
+            h = joined(dot(pr[...], bs[:, n : n + CHUNK]), PIECES) * (top_r * (1.0 / TOP))
             for i in range(CHUNK // LOC):
                 at = slice(n + i * LOC, n + (i + 1) * LOC)
                 t = n // LOC + i
@@ -421,8 +428,8 @@
                 vm((rows, ghosts), F8),
                 vm((rows, ghosts), F8),
                 vm((rows, ghosts), F8),
-                vm((rows, width), F8),
-                vm((rows, width), F8),
+                vm((PRODUCT_PIECES * states, width), F8),
+                vm((PRODUCT_PIECES * states, width), F8),
                 vm((states, width), F32),
                 vm((cells * states, 2 * LOC), BF16),
                 vm((cells * states, 2 * LOC), BF16),

time: 69.4 us -> 69 us (level)
  no operation moved by 1% of the time
where the time goes in v4:
time: 69 us; the launch traced here: 68.9 us
  Pallas kernels  68.2 us (99%)
    pallas_call x1, Pallas kernels, per_device(): pl.pallas_call(body, name='chebyshev_step', out_shape=(jax.ShapeDtypeStru...  66.6 us
    pallas_call x1, Pallas kernels, per_device(): pl.pallas_call(write_out, name='outputs', out_shape=(jax.ShapeDtypeStruct...  1.68 us

profile of v4, /device:TPU:4, one launch (start us, length us, event | category | flops | bytes accessed | tf_op | source)
XLA Modules:
  0.0 68.9 jit_solution(9167008131608658332)
XLA Ops:
  0.6 66.6 %chebyshev_step.1 = (f32[32,2048]{1,0:T(8,128)}, f32[64,128]{1,0:T(8,128)}) custom-call(f32[32,2048]{1,0:T(8,128)} %refs_0_.1, f32[16,128]{1,0:T(8,128)} %bitcast.5, f32[1,32]{1,0:T(1,128)} %bitcast.7, s32[32,125]{1,0:T(8,128)} %bitcast.4, s32[4,128]{1,0:T(4,128)} %bitcast.6, bf16[256,256]{1,0:T(8,128)(2,1)} %constant.2.clone.refs_5_), custom_call_target="tpu_custom_call" | custom-call | tf_op jit(solution)/shard_map/chebyshev_step/pallas_call | solution.py:406
  67.2 1.7 %outputs.1 = (f32[32,2048]{1,0:T(8,128)}, f32[32,128]{1,0:T(8,128)}, f32[32,128]{1,0:T(8,128)}) custom-call(f32[32,2048]{1,0:T(8,128)} %get-tuple-element.5.filt, f32[64,128]{1,0:T(8,128)} %get-tuple-element.6.total), custom_call_target="tpu_custom_call" | custom-call | tf_op jit(solution)/shard_map/outputs/pallas_call | solution.py:464

commit v5 on v4

--- a/solution.py
+++ b/solution.py
@@ -99,15 +99,26 @@
 
 def kernel(
     n_domain, n_band, nodes_total,
-    orb, pot, scl, conn, bnd, kk,
+    orb_in, pot_in, scl_in, conn_in, bnd_in, kk_in,
     filt_out, total_out,
     gt, gs, gpt, gps, bt, bs, pack, packp,
     cur, old, ay, pv, pb, pg, pr, pw, pwp, wo, xs, xsp, r2,
     bsend, grecv, rsend, rrecv,
-    fall, lhs, rhs, part, rsrecv, zbuf, tot,
+    fall, lhs, rhs, part, rsrecv, zbuf, tot, pot, scl, conn, bnd, kk, in_s,
     out_s, pk_ss, pk_rs, b_ss, b_rs, r_ss, r_rs, f_ss, f_rs, s1_ss, s1_rs, s2_ss, s2_rs, s3_ss, s3_rs,
 ):
-    states, nodes = orb.shape
+    fetches = [
+        pltpu.make_async_copy(src, dst, in_s.at[i])
+        for i, (src, dst) in enumerate(
+            (
+                (conn_in, conn), (bnd_in, bnd), (scl_in, scl), (orb_in, cur),
+                (orb_in, old), (kk_in, kk), (pot_in, pot),
+            )
+        )
+    ]
+    for fetch in fetches:
+        fetch.start()
+    states, nodes = orb_in.shape
     cells = conn.shape[0]
     ghosts = bnd.shape[0] * bnd.shape[1]
     width = cells * LOC
@@ -142,6 +153,8 @@
             src_ref=src, dst_ref=dst, send_sem=ss, recv_sem=rs, device_id=where, device_id_type=MESH
         )
 
+    for fetch in fetches[:3]:
+        fetch.wait()
     pack[0:cells, :] = jnp.full((cells, LOC), -1.0, F32)
     pack[0:cells, 0 : conn.shape[1]] = conn[...].astype(F32)
     eye = lax.broadcasted_iota(jnp.int32, (cells, cells), 0) == lax.broadcasted_iota(
@@ -182,8 +195,8 @@
     pack_copy.start()
     own_matrices(cells // 2, cells)
 
-    cur[...] = orb[...]
-    old[...] = orb[...]
+    for fetch in fetches[3:]:
+        fetch.wait()
 
     def put(dst, at, pieces):
         for p, piece in enumerate(pieces):
@@ -250,7 +263,6 @@
             fall[mb] = cur[...]
             f_near.start()
             f_far[0].start()
-            f_far[1].start()
             f_out.start()
 
         def keep(at, w):
@@ -260,6 +272,10 @@
         elements(pv, gt, slice(0, nodes), xs, own, keep)
         rsend[k] = joined(dot(pw[...], gs[:, nodes:]), PRODUCT_PIECES) * scale
         back_copy(k).start()
+
+        @pl.when(k == DEG)
+        def _():
+            f_far[1].start()
 
         @pl.when(k == 0)
         def _():
@@ -410,7 +426,7 @@
                 jax.ShapeDtypeStruct((states, nodes), F32),
                 jax.ShapeDtypeStruct((2 * states, everyone), F32),
             ),
-            in_specs=[pl.BlockSpec(memory_space=vm)] * 6,
+            in_specs=[pl.BlockSpec(memory_space=pl.ANY)] * 6,
             out_specs=(pl.BlockSpec(memory_space=pl.ANY), pl.BlockSpec(memory_space=vm)),
             scratch_shapes=[
                 vm((nodes + ghosts, width), F8),
@@ -445,6 +461,12 @@
                 vm((8, 8, everyone), F32),
                 vm((n_domain // 8, 8, everyone), F32),
                 vm((8, 8, everyone), F32),
+                vm((nodes // LOC, LOC), F32),
+                vm((1, cells), F32),
+                vm((cells, connectivity.shape[0]), jnp.int32),
+                vm((ghosts // LOC, LOC), jnp.int32),
+                vm((2 * LOC, 2 * LOC), BF16),
+                dma((7,)),
                 dma, dma, dma,
                 dma((DEG + 1,)), dma((DEG + 1,)), dma((DEG + 1,)), dma((DEG + 1,)),
                 dma((5,)), dma((5,)),

time: 69 us -> 68.3 us (0.990)
  Pallas kernels: 68.2 us -> 67.5 us
    pallas_call x1, Pallas kernels: 66.6 us -> 65.8 us  [per_device(): pl.pallas_call(body, name='chebyshev_step', out_shape=(jax.ShapeDtypeStru...]
where the time goes in v5:
time: 68.3 us; the launch traced here: 68.1 us
  Pallas kernels  67.5 us (99%)
    pallas_call x1, Pallas kernels, per_device(): pl.pallas_call(body, name='chebyshev_step', out_shape=(jax.ShapeDtypeStru...  65.8 us
    pallas_call x1, Pallas kernels, per_device(): pl.pallas_call(write_out, name='outputs', out_shape=(jax.ShapeDtypeStruct...  1.68 us

profile of v5, /device:TPU:4, one launch (start us, length us, event | category | flops | bytes accessed | tf_op | source)
XLA Modules:
  0.0 68.1 jit_solution(3397358518455944431)
XLA Ops:
  0.6 65.8 %chebyshev_step.1 = (f32[32,2048]{1,0:T(8,128)}, f32[64,128]{1,0:T(8,128)}) custom-call(f32[32,2048]{1,0:T(8,128)} %refs_0_.1, f32[16,128]{1,0:T(8,128)} %bitcast.5, f32[1,32]{1,0:T(1,128)} %bitcast.7, s32[32,125]{1,0:T(8,128)} %bitcast.4, s32[4,128]{1,0:T(4,128)} %bitcast.6, bf16[256,256]{1,0:T(8,128)(2,1)} %constant.2.clone.refs_5_), custom_call_target="tpu_custom_call" | custom-call | tf_op jit(solution)/shard_map/chebyshev_step/pallas_call | solution.py:422
  66.4 1.7 %outputs.1 = (f32[32,2048]{1,0:T(8,128)}, f32[32,128]{1,0:T(8,128)}, f32[32,128]{1,0:T(8,128)}) custom-call(f32[32,2048]{1,0:T(8,128)} %get-tuple-element.5.filt, f32[64,128]{1,0:T(8,128)} %get-tuple-element.6.total), custom_call_target="tpu_custom_call" | custom-call | tf_op jit(solution)/shard_map/outputs/pallas_call | solution.py:486

commit v6 on v5

--- a/solution.py
+++ b/solution.py
@@ -249,6 +249,9 @@
 
     @pl.loop(0, DEG + 1)
     def _(k):
+        first = (k == 0).astype(F32)
+        alpha = (2.0 - first) / SPREAD
+        beta = 1.0 - first
         y = cur[...]
         top = row_max(y)
         scale, inverse = top * (1.0 / TOP), TOP / top
@@ -304,7 +307,15 @@
         )
         for n in range(0, nodes, CHUNK):
             at = slice(n, n + CHUNK)
-            ay[:, at] = joined(dot(pw[...], gs[:, at]), PRODUCT_PIECES) * scale_b
+            h = joined(dot(pw[...], gs[:, at]), PRODUCT_PIECES) * scale_b
+            for i in range(CHUNK // LOC):
+                at = slice(n + i * LOC, n + (i + 1) * LOC)
+                t = n // LOC + i
+                v = cur[:, at]
+                full = h[:, i * LOC : (i + 1) * LOC] + pot[t : t + 1, :] * v
+                ay[:, at] = full
+                cur[:, at] = alpha * (full - CENTRE * v) - beta * old[:, at]
+                old[:, at] = v
 
         @pl.when(k == DEG)
         def _():
@@ -315,19 +326,11 @@
         shared = rrecv[k] + r2[...]
         top_r = row_max(shared)
         put(pr, slice(0, ghosts), cut(shared * (TOP / top_r), PIECES))
-        first = (k == 0).astype(F32)
-        alpha = (2.0 - first) / SPREAD
-        beta = 1.0 - first
         for n in range(0, nodes, CHUNK):
+            at = slice(n, n + CHUNK)
             h = joined(dot(pr[...], bs[:, n : n + CHUNK]), PIECES) * (top_r * (1.0 / TOP))
-            for i in range(CHUNK // LOC):
-                at = slice(n + i * LOC, n + (i + 1) * LOC)
-                t = n // LOC + i
-                v = cur[:, at]
-                full = ay[:, at] + h[:, i * LOC : (i + 1) * LOC] + pot[t : t + 1, :] * v
-                ay[:, at] = full
-                cur[:, at] = alpha * (full - CENTRE * v) - beta * old[:, at]
-                old[:, at] = v
+            ay[:, at] = ay[:, at] + h
+            cur[:, at] = cur[:, at] + alpha * h
 
     f_far[1].wait_recv()
     f_pass[1].start()

time: 68.3 us -> 68.2 us (level)
  no operation moved by 1% of the time
where the time goes in v6:
time: 68.2 us; the launch traced here: 68 us
  Pallas kernels  67.4 us (99%)
    pallas_call x1, Pallas kernels, per_device(): pl.pallas_call(body, name='chebyshev_step', out_shape=(jax.ShapeDtypeStru...  65.7 us
    pallas_call x1, Pallas kernels, per_device(): pl.pallas_call(write_out, name='outputs', out_shape=(jax.ShapeDtypeStruct...  1.68 us

profile of v6, /device:TPU:4, one launch (start us, length us, event | category | flops | bytes accessed | tf_op | source)
XLA Modules:
  0.0 68.0 jit_solution(7262558706764038644)
XLA Ops:
  0.6 65.7 %chebyshev_step.1 = (f32[32,2048]{1,0:T(8,128)}, f32[64,128]{1,0:T(8,128)}) custom-call(f32[32,2048]{1,0:T(8,128)} %refs_0_.1, f32[16,128]{1,0:T(8,128)} %bitcast.5, f32[1,32]{1,0:T(1,128)} %bitcast.7, s32[32,125]{1,0:T(8,128)} %bitcast.4, s32[4,128]{1,0:T(4,128)} %bitcast.6, bf16[256,256]{1,0:T(8,128)(2,1)} %constant.2.clone.refs_5_), custom_call_target="tpu_custom_call" | custom-call | tf_op jit(solution)/shard_map/chebyshev_step/pallas_call | solution.py:425
  66.3 1.7 %outputs.1 = (f32[32,2048]{1,0:T(8,128)}, f32[32,128]{1,0:T(8,128)}, f32[32,128]{1,0:T(8,128)}) custom-call(f32[32,2048]{1,0:T(8,128)} %get-tuple-element.5.filt, f32[64,128]{1,0:T(8,128)} %get-tuple-element.6.total), custom_call_target="tpu_custom_call" | custom-call | tf_op jit(solution)/shard_map/outputs/pallas_call | solution.py:489
